TPU v7x, 32 devices: a whole 2x2x4 slice. The times are simulated.
32 devices in a mesh: grp: 2 (over y), feat: 4 (over z), samp: 4 (over x, core).
Axes of the slice: x: 2, y: 2, z: 4, core: 2. Of those that a mesh axis runs over, the one named last changes fastest.
Arguments:
- embeddings: bfloat16 [8192, 1024], P(('grp', 'samp')), parts along dimension 0, may hold values from -6 to 6
- sign_bits: int32 [4096], P('feat'), may hold values 0 or 1
- perms: int32 [4, 1024], P('feat'), may hold values from 0 to 1023, each once within a row
- gauss: float32 [4096], P('feat'), may hold values from -4 to 4
- scale: float32 [4096], P('feat'), may hold values from 0.5 to 2
- phase: float32 [4096], P('feat'), may hold values from -3.140625 to 3.140625
- basis: float32 [128, 4096], P('grp', 'feat'), parts along dimension 0, may hold values from -40 to 40
Outputs:
- basis_out: float32 [128, 4096], P('grp', 'feat'), parts along dimension 0
- projections: float32 [128, 4096], P('grp', 'samp'), parts along dimension 0
There are 2 independent parts, one for each index of `grp`. A program takes and returns all parts, laid end to end along the dimension named above; an argument that names none is the same for every part. Nothing has to cross between parts.
Inputs may be any that keep to these rules, and one draw needn't show every extreme that they name: Each row of perms names every number of 0 to 1023 once.
All inputs are finite; a program needn't handle non-finite values. No bound on the sum of `sign_bits` on one device may be relied on, other than what follows from the above.
Results may differ from a plain program's by a relative error of at most 0.0057.
Values sent between devices are 32-bit elements; how exact they have to be, the bound alone decides.
A program may use at most 64 MiB of HBM per device.

v0:
```python
import math

import jax
import jax.numpy as jnp
from jax import lax
from jax.sharding import PartitionSpec as P


def sylvester(width):
    indices = lax.iota(jnp.int32, width)
    parity = jnp.zeros((width, width), jnp.int32)
    for position in range(width.bit_length() - 1):
        row_bits = jnp.right_shift(indices[:, None], position) & 1
        col_bits = jnp.right_shift(indices[None, :], position) & 1
        parity = parity + row_bits * col_bits
    return jnp.where(parity % 2 == 0, 1.0, -1.0).astype(jnp.bfloat16)


def cholesky_step(grown, total):
    local_gram = jnp.dot(grown, grown.T, precision=lax.Precision.HIGHEST)
    gram = lax.psum(local_gram, "feat")
    lower = jnp.linalg.cholesky(gram / total)
    return jax.scipy.linalg.solve_triangular(lower, grown, lower=True)


def local(embeddings, sign_bits, perms, gauss, scale, phase, basis):
    width = embeddings.shape[1]
    rows = embeddings.shape[0]
    table = sylvester(width)
    features_total = width * lax.axis_size("feat")
    span_total = rows * lax.axis_size("samp")
    signs = (2 * sign_bits - 1).astype(jnp.bfloat16)
    first = jnp.dot(embeddings * signs, table, preferred_element_type=jnp.float32).astype(
        jnp.bfloat16
    )
    reorder = (lax.iota(jnp.int32, width)[:, None] == perms[0][None, :]).astype(jnp.bfloat16)
    picked = jnp.dot(first, reorder, preferred_element_type=jnp.float32)
    mixed = (picked * gauss).astype(jnp.bfloat16)
    freq = jnp.dot(mixed, table, preferred_element_type=jnp.float32) * scale / width + phase
    features = (math.sqrt(2.0) * jnp.cos(freq)).astype(jnp.bfloat16)
    basis_low = basis.astype(jnp.bfloat16)
    partial_scores = lax.dot_general(
        basis_low, features, (((1,), (1,)), ((), ())), preferred_element_type=jnp.float32
    )
    summed = lax.psum(partial_scores, "feat")
    projections = summed / math.sqrt(features_total)
    proj_low = projections.astype(jnp.bfloat16)
    update_part = jnp.dot(proj_low, features, preferred_element_type=jnp.float32)
    update = lax.psum(update_part, "samp")
    grown = basis + update / math.sqrt(span_total)
    basis_out = cholesky_step(grown, features_total)
    return (basis_out, projections)


def solution(mesh):
    placed = (
        P(("grp", "samp"), None),
        P("feat"),
        P("feat", None),
        P("feat"),
        P("feat"),
        P("feat"),
        P("grp", "feat"),
    )
    return jax.shard_map(
        local,
        mesh=mesh,
        in_specs=placed,
        out_specs=(P("grp", "feat"), P("grp", "samp")),
        check_vma=False,
    )
```

profile of v0, /device:TPU:0, one launch (start us, length us, event | category | flops | bytes accessed | tf_op | source)
XLA Modules:
  0.0 159.9 jit_solution(12361996061334306493)
XLA Ops:
  7.2 0.0 all-reduce.3.cloned.1.call-start
  7.3 0.7 add_convert_fusion
  8.0 1.5 iota_compare_fusion.7
  9.5 0.0 copy-start.2
  9.5 0.0 copy-start.3
  9.5 12.2 %fusion.2 = f32[1024,1024]{1,0:T(8,128)} fusion(bf16[1024,1024]{1,0:T(8,128)(2,1)} %param.7, bf16[1024]{0:T(1024)(128)(2,1)S(1)} %add_convert_fusion, s32[1024]{0:T(1024)S(1)} %get-tuple-element.2, s32[1024]{0:T(1024)S(1)} %get-tuple-element.3, s32[1024]{0:T(1024)S(1)} %get-tuple-element.4, s32[1024]{0:T(1024)S(1)} %get-tuple-element.5, ...), kind=kOutput, calls=%fused_computation.9 | convolution fusion | flops 4331667456 | bytes 7383040 | tf_op jit(solution)/shard_map/dot_general | solution.py:37
  21.7 22.2 %multiply_convert_fusion = bf16[1024,1024]{1,0:T(8,128)(2,1)S(1)} fusion(f32[1024,1024]{1,0:T(8,128)} %fusion.2, f32[1024]{0:T(1024)S(1)} %copy-done.2, f32[1024]{0:T(1024)S(1)} %copy-done.3, f32[1024]{0:T(1024)S(1)} %copy-done.4, s32[1024]{0:T(1024)S(1)} %get-tuple-element.2, s32[1024]{0:T(1024)S(1)} %get-tuple-element.3, s32[1024]{0:T(1024)S(1)} %get-tuple-element.4, ...), kind=kOutput, calls=%fused_computation.5 | convolution fusion | flops 2189426688 | bytes 6344704 | tf_op jit(solution)/shard_map/dot_general | solution.py:39
  44.0 1.5 convolution_bitcast_fusion
  45.4 0.0 all-reduce.3.cloned.1.call-update
  45.5 0.0 all-reduce.5.cloned.1.call-start
  45.5 38.1 %all-reduce.3.cloned.1.call-done = f32[64,1024]{1,0:T(8,128)} async-done(((f32[64,1024]{1,0:T(8,128)}), f32[64,1024]{1,0:T(8,128)}) %all-reduce.3.cloned.1.call-update) | async-done | bytes 262160 | tf_op jit(solution)/shard_map/psum | solution.py:45
  83.6 1.0 broadcast_multiply_fusion
  84.6 0.0 copy-start.1
  84.6 1.2 fusion.14
  85.8 0.0 all-reduce.5.cloned.1.call-update
  85.8 32.5 %all-reduce.5.cloned.1.call-done = f32[64,1024]{1,0:T(8,128)} async-done(((f32[64,1024]{1,0:T(8,128)}), f32[64,1024]{1,0:T(8,128)}) %all-reduce.5.cloned.1.call-update) | async-done | bytes 262160 | tf_op jit(solution)/shard_map/psum | solution.py:49
  118.4 1.4 fusion.18
  119.8 19.0 %psum.23 = f32[64,64]{0,1:T(8,128)S(1)} all-reduce(f32[64,64]{0,1:T(8,128)S(1)} %fusion.18), channel_id=1, replica_groups=mesh['grp'=2,'feat'=4,'samp'=4] {'feat'}, use_global_device_ids=true, to_apply=%region_2.3 | all-reduce | flops 4096 | bytes 32768 | tf_op jit(solution)/shard_map/psum | solution.py:21
  138.8 0.1 copy.10
  138.9 5.8 %cholesky.16 = f32[64,64]{1,0:T(8,128)S(1)} custom-call(f32[64,64]{1,0:T(8,128)S(1)} %fusion.21), custom_call_target="Cholesky" | custom-call | tf_op jit(solution)/shard_map/jit(cholesky)/cholesky | solution.py:22
  144.7 0.6 compare_reduce_fusion
  145.4 0.7 fusion.19
  146.1 4.9 %custom-call.7 = f32[1,64,64]{1,2,0:T(8,128)S(1)} custom-call(f32[1,64,64]{2,1,0:T(8,128)S(1)} %fusion.19), custom_call_target="InvertDiagBlocksLowerTriangular" | custom-call | tf_op jit(solution)/shard_map/jit(_solve_triangular)/triangular_solve | solution.py:23
  150.9 2.1 %fusion.17 = f32[64,1024]{1,0:T(8,128)} fusion(f32[64,1024]{1,0:T(8,128)S(1)} %copy-done, f32[64,1024]{1,0:T(8,128)} %all-reduce.5.cloned.1.call-done, f32[1,64,64]{1,2,0:T(8,128)S(1)} %custom-call.7), kind=kOutput, calls=%fused_computation.22 | convolution fusion | flops 50462720 | bytes 802816 | tf_op jit(solution)/shard_map/jit(_solve_triangular)/triangular_solve | solution.py:23
  (15 shorter events, 0.1 us)
Async XLA Ops:
  7.2 76.5 %all-reduce.3.cloned.1.call-start = ((), (), s32[]{:S(2)}) async-start(), calls=%async_computation | async-start | bytes 524288 | tf_op jit(solution)/shard_map/psum | solution.py:45
  9.5 12.3 %copy-start.2 = (f32[1024]{0:T(1024)S(1)}, f32[1024]{0:T(1024)}, u32[]{:S(2)}) copy-start(f32[1024]{0:T(1024)} %param.12) | copy-start | bytes 12292
  9.5 12.3 %copy-start.3 = (f32[1024]{0:T(1024)S(1)}, f32[1024]{0:T(1024)}, u32[]{:S(2)}) copy-start(f32[1024]{0:T(1024)} %param.11) | copy-start | bytes 12292
  9.5 12.3 %copy-start.4 = (f32[1024]{0:T(1024)S(1)}, f32[1024]{0:T(1024)}, u32[]{:S(2)}) copy-start(f32[1024]{0:T(1024)} %param.10) | copy-start | bytes 12292
  21.7 22.2 %copy-start = (f32[64,1024]{1,0:T(8,128)S(1)}, f32[64,1024]{1,0:T(8,128)}, u32[]{:S(2)}) copy-start(f32[64,1024]{1,0:T(8,128)} %param.13) | copy-start | bytes 786436
  45.5 72.9 %all-reduce.5.cloned.1.call-start = ((), (), s32[]{:S(2)}) async-start(), calls=%async_computation.1 | async-start | bytes 524288 | tf_op jit(solution)/shard_map/psum | solution.py:49
  84.6 68.4 %copy-start.1 = (f32[64,1024]{1,0:T(8,128)}, f32[64,1024]{1,0:T(8,128)S(1)}, u32[]{:S(2)}) copy-start(f32[64,1024]{1,0:T(8,128)S(1)} %broadcast_multiply_fusion) | copy-start | bytes 786436
Sparse Core Ops, SparseCore 0:
  45.6 37.9 all-reduce.2
  86.6 31.6 all-reduce.4
where the time goes:
time: 160 us
  waiting for transfers between devices  70.7 us (44%)
  matrix products  40.6 us (25%)
  blocking collectives  19 us (12%)
  other arithmetic  15.3 us (10%)
  between operations  14.2 us (9%)
    psum x1, waiting for transfers between devices, local(): summed = lax.psum(partial_scores, 'feat')  38.1 us
    psum x1, waiting for transfers between devices, local(): update = lax.psum(update_part, 'samp')  32.5 us
    dot_general x1, matrix products, local(): jnp.dot(mixed, table, preferred_element_type=jnp.float32) * scale / width  22.2 us
    psum x1, blocking collectives, cholesky_step(): gram = lax.psum(local_gram, 'feat')  19 us
    dot_general x1, matrix products, local(): picked = jnp.dot(first, reorder, preferred_element_type=jnp.float32)  12.2 us
    another operation x3, other arithmetic, cholesky_step(): lower = jnp.linalg.cholesky(gram / total)  6.52 us
    another operation x2, other arithmetic, cholesky_step(): return jax.scipy.linalg.solve_triangular(lower, grown, lower=True)  5.55 us
  transfers between devices with their start and end apart: 2, of which 2 were waited for; matrix products, arithmetic and copies ran while one was open for 0% of the time, Pallas kernels for 0%

commit v1 on v0

v1 whole, which is shorter than its diff:
```python
import functools
import math

import jax
import jax.numpy as jnp
import numpy as np
from jax import lax
from jax.experimental import pallas as pl
from jax.experimental.pallas import tpu as pltpu
from jax.sharding import PartitionSpec as P

MESH = pl.DeviceIdType.MESH
BLOCK = 256
HIGHEST = lax.Precision.HIGHEST


def cosine_coefficients(degree):
    nodes = np.cos(np.pi * (np.arange(400) + 0.5) / 400)
    squares = (nodes + 1) / 8
    fitted = np.polynomial.Chebyshev.fit(
        squares, np.cos(2 * np.pi * np.sqrt(squares)), degree, domain=[0, 0.25]
    )
    return [float(c) * math.sqrt(2.0) for c in fitted.convert(kind=np.polynomial.Polynomial).coef]


COS = cosine_coefficients(6)


def parity_sign(bits):
    for shift in (8, 4, 2, 1):
        bits = bits ^ jnp.right_shift(bits, shift)
    return (1 - 2 * (bits & 1)).astype(jnp.float32)


def scaled_cosine(turns):
    rest = turns - jnp.round(turns)
    square = rest * rest
    total = jnp.full_like(square, COS[-1])
    for c in COS[-2::-1]:
        total = total * square + c
    return total


def transform(blocks):
    stride = 1
    while stride < len(blocks):
        result = list(blocks)
        for i in range(len(blocks)):
            if not i & stride:
                result[i] = blocks[i] + blocks[i + stride]
                result[i + stride] = blocks[i] - blocks[i + stride]
        blocks = result
        stride *= 2
    return blocks


def inverse_factor(gram):
    size = gram.shape[0]
    row = lax.broadcasted_iota(jnp.int32, (8, size), 0)
    lane = lax.broadcasted_iota(jnp.int32, (8, size), 1)
    width = 2 * size
    sub = lax.broadcasted_iota(jnp.int32, (8, width), 0)
    groups = [
        jnp.concatenate(
            [(lane == row + 8 * g).astype(jnp.float32), gram[8 * g : 8 * g + 8]], axis=1
        )
        for g in range(size // 8)
    ]
    pivots = [jnp.ones((8, width), jnp.float32) for _ in groups]
    step = 4
    for first in range(0, size, step):
        own = first // 8
        at = first % 8
        live = range(own, size // 8)
        rows = [
            jnp.broadcast_to(groups[own][at + k : at + k + 1], (8, width)) for k in range(step)
        ]
        cols = [
            {
                g: jnp.broadcast_to(
                    groups[g][:, size + first + k : size + first + k + 1], (8, width)
                )
                for g in live
            }
            for k in range(step)
        ]
        cross = [
            [
                jnp.broadcast_to(cols[m][own][at + k : at + k + 1], (8, width))
                for m in range(step)
            ]
            for k in range(step)
        ]
        for k in range(step):
            inverse = 1.0 / cross[k][k]
            pivots[own] = jnp.where(sub == at + k, cross[k][k], pivots[own])
            for later in range(k + 1, step):
                factor = cross[later][k] * inverse
                rows[later] = rows[later] - factor * rows[k]
                share = cross[k][later] * inverse
                for g in live:
                    cols[later][g] = cols[later][g] - share * cols[k][g]
                for m in range(k + 1, step):
                    cross[later][m] = cross[later][m] - factor * cross[k][m]
            for g in live:
                weight = cols[k][g] * inverse
                if g == own:
                    weight = jnp.where(sub > at + k, weight, 0.0)
                groups[g] = groups[g] - weight * rows[k]
    scaled = [g / jnp.sqrt(p) for g, p in zip(groups, pivots)]
    return jnp.concatenate(scaled, axis=0)[:, :size]


def kernel(
    feats, samps, emb, bits, perm, gauss, scale, phase, basis, out, scores_out,
    table, small, features, score_send, score_recv, proj, upd_send, upd_recv, grown,
    gram_send, gram_recv,
    s1, r1, s2, r2, s3, r3, s4, r4, s5, r5,
):
    me = lax.axis_index("feat")
    my = lax.axis_index("samp")
    rows, width = emb.shape
    order = basis.shape[0]
    chunk = rows // feats
    span = width // samps
    barrier = pltpu.get_barrier_semaphore()
    for d in range(1, feats):
        pl.semaphore_signal(
            barrier, inc=1, device_id={"feat": lax.rem(me + d, feats)}, device_id_type=MESH
        )
    for d in range(1, samps):
        pl.semaphore_signal(
            barrier, inc=1, device_id={"samp": lax.rem(my + d, samps)}, device_id_type=MESH
        )

    places = perm[...]
    base = parity_sign(lax.broadcasted_iota(jnp.int32, (128, width), 0) & places & 127).astype(
        jnp.bfloat16
    )
    for a in range(width // 128):
        flips = parity_sign(jnp.right_shift(places, 7) & a).astype(jnp.bfloat16)
        table[a * 128 : (a + 1) * 128, :] = base * flips
    square = (BLOCK, BLOCK)
    small[...] = parity_sign(
        lax.broadcasted_iota(jnp.int32, square, 0) & lax.broadcasted_iota(jnp.int32, square, 1)
    ).astype(jnp.bfloat16)
    signs = (2 * bits[...] - 1).astype(jnp.float32).astype(jnp.bfloat16)
    gains = gauss[...]
    rate = scale[...] * (1.0 / (2.0 * math.pi * width))
    offset = phase[...] * (1.0 / (2.0 * math.pi))
    basis_low = basis[...].astype(jnp.bfloat16)

    pl.semaphore_wait(barrier, feats + samps - 2)

    def copy(src, dst, send, recv, axis, to):
        return pltpu.make_async_remote_copy(
            src_ref=src, dst_ref=dst, send_sem=send, recv_sem=recv,
            device_id={axis: to}, device_id_type=MESH,
        )

    def score_copy(to):
        return copy(score_send.at[to], score_recv.at[me], s1.at[to], r1.at[me], "feat", to)

    def chunk_step(i, carry):
        at = lax.rem(me + 1 + i, feats)
        where = pl.ds(pl.multiple_of(at * chunk, chunk), chunk)
        signed = emb[where, :] * signs
        parts = []
        for n in range(width // BLOCK):
            cols = slice(n * BLOCK, (n + 1) * BLOCK)
            first = jnp.dot(signed, table[:, cols], preferred_element_type=jnp.float32)
            first = first.astype(jnp.bfloat16).astype(jnp.float32)
            mixed = (first * gains[:, cols]).astype(jnp.bfloat16)
            parts.append(jnp.dot(mixed, small[...], preferred_element_type=jnp.float32))
        for n, part in enumerate(transform(parts)):
            cols = slice(n * BLOCK, (n + 1) * BLOCK)
            turns = part * rate[:, cols] + offset[:, cols]
            features[where, cols] = scaled_cosine(turns).astype(jnp.bfloat16)
        score_send[at] = lax.dot_general(
            basis_low, features[where, :], (((1,), (1,)), ((), ())),
            preferred_element_type=jnp.float32,
        )

        @pl.when(i < feats - 1)
        def _():
            score_copy(at).start()

        return carry

    lax.fori_loop(0, feats, chunk_step, 0)

    total = score_send[me]
    for d in range(1, feats):
        source = lax.rem(me + d, feats)
        copy(
            score_send.at[source], score_recv.at[source], s1.at[source], r1.at[source],
            "feat", source,
        ).wait_recv()
        total = total + score_recv[source]
    proj[me] = total * (1.0 / math.sqrt(width * feats))

    def proj_copy(slot, to):
        return copy(proj.at[slot], proj.at[slot], s2.at[to], r2.at[slot], "feat", to)

    for d in range(1, feats):
        proj_copy(me, lax.rem(me + d, feats)).start()

    def add_rows(slot, first):
        where = pl.ds(pl.multiple_of(slot * chunk, chunk), chunk)
        low = proj[slot].astype(jnp.bfloat16)
        for q in range(samps):
            term = jnp.dot(
                low, features[where, q * span : (q + 1) * span],
                preferred_element_type=jnp.float32,
            )
            upd_send[q] = term if first else upd_send[q] + term

    add_rows(me, True)
    for d in range(1, feats):
        source = lax.rem(me + d, feats)
        proj_copy(source, source).wait_recv()
        add_rows(source, False)

    def upd_copy(to):
        return copy(upd_send.at[to], upd_recv.at[my], s3.at[to], r3.at[my], "samp", to)

    for d in range(1, samps):
        upd_copy(lax.rem(my + d, samps)).start()
    for slot in range(feats):
        scores_out[:, slot * chunk : (slot + 1) * chunk] = proj[slot]
    total = upd_send[my]
    for d in range(1, samps):
        source = lax.rem(my + d, samps)
        copy(
            upd_send.at[source], upd_recv.at[source], s3.at[source], r3.at[source],
            "samp", source,
        ).wait_recv()
        total = total + upd_recv[source]
    own_cols = pl.ds(pl.multiple_of(my * span, span), span)
    grown[my] = basis[:, own_cols] + total * (1.0 / math.sqrt(rows * samps))

    def grown_copy(slot, to):
        return copy(grown.at[slot], grown.at[slot], s4.at[to], r4.at[slot], "samp", to)

    for d in range(1, samps):
        grown_copy(my, lax.rem(my + d, samps)).start()

    def gram_of(slot):
        block = grown[slot]
        return lax.dot_general(
            block, block, (((1,), (1,)), ((), ())), precision=HIGHEST,
            preferred_element_type=jnp.float32,
        )

    gram = gram_of(my)
    for d in range(1, samps):
        source = lax.rem(my + d, samps)
        grown_copy(source, source).wait_recv()
        gram = gram + gram_of(source)

    half = order // 2
    packed = jnp.concatenate([gram[:half], gram[half:]], axis=1)
    gram_send[...] = packed

    def gram_copy(slot, to):
        return copy(gram_send, gram_recv.at[slot], s5.at[to], r5.at[slot], "feat", to)

    for d in range(1, feats):
        gram_copy(me, lax.rem(me + d, feats)).start()
    gram_recv[me] = packed
    for d in range(1, feats):
        source = lax.rem(me + d, feats)
        gram_copy(source, source).wait_recv()
    packed = gram_recv[0]
    for slot in range(1, feats):
        packed = packed + gram_recv[slot]
    packed = packed * (1.0 / (width * feats))
    gram = jnp.concatenate([packed[:, :order], packed[:, order:]], axis=0)
    inverse = inverse_factor(gram)
    for q in range(samps):
        out[:, q * span : (q + 1) * span] = jnp.dot(
            inverse, grown[q], precision=HIGHEST, preferred_element_type=jnp.float32
        )

    for d in range(1, feats):
        to = lax.rem(me + d, feats)
        score_copy(to).wait_send()
        proj_copy(me, to).wait_send()
        gram_copy(me, to).wait_send()
    for d in range(1, samps):
        to = lax.rem(my + d, samps)
        upd_copy(to).wait_send()
        grown_copy(my, to).wait_send()


def fused(feats, samps, embeddings, sign_bits, perms, gauss, scale, phase, basis):
    rows, width = embeddings.shape
    order = basis.shape[0]
    chunk, span = rows // feats, width // samps
    line = (1, width)
    whole = pl.BlockSpec(memory_space=pltpu.VMEM)
    f32, bf16, dma = jnp.float32, jnp.bfloat16, pltpu.SemaphoreType.DMA
    return pl.pallas_call(
        functools.partial(kernel, feats, samps),
        out_shape=(
            jax.ShapeDtypeStruct((order, width), f32),
            jax.ShapeDtypeStruct((order, rows), f32),
        ),
        in_specs=[whole] * 7,
        out_specs=(whole, whole),
        scratch_shapes=[
            pltpu.VMEM((width, width), bf16),
            pltpu.VMEM((BLOCK, BLOCK), bf16),
            pltpu.VMEM((rows, width), bf16),
            pltpu.VMEM((feats, order, chunk), f32),
            pltpu.VMEM((feats, order, chunk), f32),
            pltpu.VMEM((feats, order, chunk), f32),
            pltpu.VMEM((samps, order, span), f32),
            pltpu.VMEM((samps, order, span), f32),
            pltpu.VMEM((samps, order, span), f32),
            pltpu.VMEM((order // 2, 2 * order), f32),
            pltpu.VMEM((feats, order // 2, 2 * order), f32),
        ]
        + [dma((feats,))] * 4
        + [dma((samps,))] * 4
        + [dma((feats,))] * 2,
        compiler_params=pltpu.CompilerParams(
            collective_id=0, has_side_effects=True, vmem_limit_bytes=40 << 20
        ),
        name="oja",
    )(
        embeddings, sign_bits.reshape(line), perms.reshape(line), gauss.reshape(line),
        scale.reshape(line), phase.reshape(line), basis,
    )


def sylvester(width):
    indices = lax.iota(jnp.int32, width)
    return parity_sign(indices[:, None] & indices[None, :]).astype(jnp.bfloat16)


def general(embeddings, sign_bits, perms, gauss, scale, phase, basis):
    rows, width = embeddings.shape
    table = sylvester(width)
    features_total = width * lax.axis_size("feat")
    span_total = rows * lax.axis_size("samp")
    signs = (2 * sign_bits - 1).astype(jnp.bfloat16)
    columns = parity_sign(lax.iota(jnp.int32, width)[:, None] & perms[0][None, :]).astype(
        jnp.bfloat16
    )
    first = jnp.dot(embeddings * signs, columns, preferred_element_type=jnp.float32)
    mixed = (first.astype(jnp.bfloat16) * gauss).astype(jnp.bfloat16)
    freq = jnp.dot(mixed, table, preferred_element_type=jnp.float32) * scale / width + phase
    features = (math.sqrt(2.0) * jnp.cos(freq)).astype(jnp.bfloat16)
    partial_scores = lax.dot_general(
        basis.astype(jnp.bfloat16), features, (((1,), (1,)), ((), ())),
        preferred_element_type=jnp.float32,
    )
    projections = lax.psum(partial_scores, "feat") / math.sqrt(features_total)
    update_part = jnp.dot(
        projections.astype(jnp.bfloat16), features, preferred_element_type=jnp.float32
    )
    grown = basis + lax.psum(update_part, "samp") / math.sqrt(span_total)
    gram = lax.psum(jnp.dot(grown, grown.T, precision=HIGHEST), "feat")
    lower = jnp.linalg.cholesky(gram / features_total)
    return jax.scipy.linalg.solve_triangular(lower, grown, lower=True), projections


def solution(mesh):
    feats, samps = mesh.shape["feat"], mesh.shape["samp"]

    def local(embeddings, sign_bits, perms, gauss, scale, phase, basis):
        rows, width = embeddings.shape
        fits = (
            rows % (feats * 128) == 0
            and width % (samps * 128) == 0
            and width % BLOCK == 0
            and perms.shape[0] == 1
            and basis.shape[0] == 64
            and 1 < feats
            and 1 < samps
        )
        body = functools.partial(fused, feats, samps) if fits else general
        return body(embeddings, sign_bits, perms, gauss, scale, phase, basis)

    placed = (
        P(("grp", "samp"), None),
        P("feat"),
        P("feat", None),
        P("feat"),
        P("feat"),
        P("feat"),
        P("grp", "feat"),
    )
    return jax.shard_map(
        local,
        mesh=mesh,
        in_specs=placed,
        out_specs=(P("grp", "feat"), P("grp", "samp")),
        check_vma=False,
    )
```

time: 160 us -> 46.8 us (0.29)
  waiting for transfers between devices: 70.7 us -> 0 us
  matrix products: 40.6 us -> 0 us
  Pallas kernels: 0 us -> 38.4 us
  blocking collectives: 19 us -> 0 us
  other arithmetic: 15.3 us -> 0 us
  between operations: 14.2 us -> 0.66 us
  local copies, waits for them, and re-layouts: 0.11 us -> 7.37 us
    psum x2 -> x0, waiting for transfers between devices: 70.7 us -> none  [the longest x1 38.1 us: local(): summed = lax.psum(partial_scores, 'feat')]
    dot_general x5 -> x0, matrix products: 38.5 us -> none  [the longest x1 22.2 us: local(): jnp.dot(mixed, table, preferred_element_type=jnp.float32) * scale / width]
    pallas_call x0 -> x1, Pallas kernels: none -> 38.4 us  [fused(): pl.pallas_call(functools.partial(kernel, feats, samps), out_shape=(jax.Sh...]
    psum x1 -> x0, blocking collectives: 19 us -> none  [cholesky_step(): gram = lax.psum(local_gram, 'feat')]
    another operation x5 -> x0, other arithmetic: 12.1 us -> none  [the longest x3 6.52 us: cholesky_step(): lower = jnp.linalg.cholesky(gram / total)]
    unnamed x10 -> x16, local copies, waits for them, and re-layouts: 0.03 us -> 7.37 us
    another operation x1 -> x0, matrix products: 2.08 us -> none  [cholesky_step(): return jax.scipy.linalg.solve_triangular(lower, grown, lower=True)]
  transfers between devices with their start and end apart: 2 -> 0, of which waited for: 2 -> 0; matrix products, arithmetic and copies ran while one was open for 0% -> 0% of each run, Pallas kernels for 0% -> 0%
where the time goes in v1:
time: 46.8 us; the launch traced here: 46.5 us
  Pallas kernels  38.4 us (82%)
  local copies, waits for them, and re-layouts  7.37 us (16%)
  between operations  0.66 us (1%)
    pallas_call x1, Pallas kernels, fused(): pl.pallas_call(functools.partial(kernel, feats, samps), out_shape=(jax.Sh...  38.4 us
    unnamed x16, local copies, waits for them, and re-layouts  7.37 us

profile of v1, /device:TPU:0, one launch (start us, length us, event | category | flops | bytes accessed | tf_op | source)
XLA Modules:
  0.0 46.5 jit_solution(9101539508636255840)
XLA Ops:
  0.6 0.0 copy-start
  0.6 1.6 %copy-done = bf16[1024,1024]{1,0:T(8,128)(2,1)S(1)} copy-done((bf16[1024,1024]{1,0:T(8,128)(2,1)S(1)}, bf16[1024,1024]{1,0:T(8,128)(2,1)}, u32[]{:S(2)}) %copy-start) | copy-done | bytes 2097176
  2.2 0.0 copy-start.1
  2.2 0.9 %copy-done.1 = f32[64,1024]{1,0:T(8,128)S(1)} copy-done((f32[64,1024]{1,0:T(8,128)S(1)}, f32[64,1024]{1,0:T(8,128)}, u32[]{:S(2)}) %copy-start.1) | copy-done | bytes 262168
  3.2 0.0 copy-start.2
  3.2 0.7 %copy-done.2 = s32[1024]{0:T(1024)S(1)} copy-done((s32[1024]{0:T(1024)S(1)}, s32[1024]{0:T(1024)}, u32[]{:S(2)}) %copy-start.2) | copy-done | bytes 4120
  3.9 0.0 copy-start.3
  3.9 0.7 %copy-done.3 = s32[1,1024]{1,0:T(1,128)S(1)} copy-done((s32[1,1024]{1,0:T(1,128)S(1)}, s32[1,1024]{1,0:T(1,128)}, u32[]{:S(2)}) %copy-start.3) | copy-done | bytes 4120
  4.5 0.0 copy-start.4
  4.6 0.7 %copy-done.4 = f32[1024]{0:T(1024)S(1)} copy-done((f32[1024]{0:T(1024)S(1)}, f32[1024]{0:T(1024)}, u32[]{:S(2)}) %copy-start.4) | copy-done | bytes 4120
  5.2 0.0 copy-start.5
  5.2 0.7 %copy-done.5 = f32[1024]{0:T(1024)S(1)} copy-done((f32[1024]{0:T(1024)S(1)}, f32[1024]{0:T(1024)}, u32[]{:S(2)}) %copy-start.5) | copy-done | bytes 4120
  5.9 0.0 copy-start.6
  5.9 0.7 %copy-done.6 = f32[1024]{0:T(1024)S(1)} copy-done((f32[1024]{0:T(1024)S(1)}, f32[1024]{0:T(1024)}, u32[]{:S(2)}) %copy-start.6) | copy-done | bytes 4120
  6.6 38.4 %oja.1 = (f32[64,1024]{1,0:T(8,128)S(1)}, f32[64,1024]{1,0:T(8,128)S(1)}) custom-call(bf16[1024,1024]{1,0:T(8,128)(2,1)S(1)} %copy-done, s32[1,1024]{1,0:T(1,128)S(1)} %bitcast.4, s32[1,1024]{1,0:T(1,128)S(1)} %copy-done.3, f32[1,1024]{1,0:T(1,128)S(1)} %bitcast.5, f32[1,1024]{1,0:T(1,128)S(1)} %bitcast.6, f32[1,1024]{1,0:T(1,128)S(1)} %bitcast.7, ...), custom_call_target="tpu_custom_call" | custom-call | tf_op jit(solution)/shard_map/oja/pallas_call | solution.py:303
  45.1 0.7 %copy.11 = f32[64,1024]{1,0:T(8,128)} copy(f32[64,1024]{1,0:T(8,128)S(1)} %get-tuple-element.4) | data formatting | bytes 524288
  45.8 0.7 %copy.12 = f32[64,1024]{1,0:T(8,128)} copy(f32[64,1024]{1,0:T(8,128)S(1)} %get-tuple-element.5) | data formatting | bytes 524288
Async XLA Ops:
  0.6 1.6 %copy-start = (bf16[1024,1024]{1,0:T(8,128)(2,1)S(1)}, bf16[1024,1024]{1,0:T(8,128)(2,1)}, u32[]{:S(2)}) copy-start(bf16[1024,1024]{1,0:T(8,128)(2,1)} %emb.1) | copy-start | bytes 6291460
  2.2 0.9 %copy-start.1 = (f32[64,1024]{1,0:T(8,128)S(1)}, f32[64,1024]{1,0:T(8,128)}, u32[]{:S(2)}) copy-start(f32[64,1024]{1,0:T(8,128)} %basis.1) | copy-start | bytes 786436
  3.2 0.7 %copy-start.2 = (s32[1024]{0:T(1024)S(1)}, s32[1024]{0:T(1024)}, u32[]{:S(2)}) copy-start(s32[1024]{0:T(1024)} %param.8) | copy-start | bytes 12292
  3.9 0.7 %copy-start.3 = (s32[1,1024]{1,0:T(1,128)S(1)}, s32[1,1024]{1,0:T(1,128)}, u32[]{:S(2)}) copy-start(s32[1,1024]{1,0:T(1,128)} %perm.1) | copy-start | bytes 12292
  4.5 0.7 %copy-start.4 = (f32[1024]{0:T(1024)S(1)}, f32[1024]{0:T(1024)}, u32[]{:S(2)}) copy-start(f32[1024]{0:T(1024)} %param.10) | copy-start | bytes 12292
  5.2 0.7 %copy-start.5 = (f32[1024]{0:T(1024)S(1)}, f32[1024]{0:T(1024)}, u32[]{:S(2)}) copy-start(f32[1024]{0:T(1024)} %param.11) | copy-start | bytes 12292
  5.9 0.7 %copy-start.6 = (f32[1024]{0:T(1024)S(1)}, f32[1024]{0:T(1024)}, u32[]{:S(2)}) copy-start(f32[1024]{0:T(1024)} %param.12) | copy-start | bytes 12292

commit v2 on v1

--- a/solution.py
+++ b/solution.py
@@ -67,55 +67,49 @@
         for g in range(size // 8)
     ]
     pivots = [jnp.ones((8, width), jnp.float32) for _ in groups]
-    step = 4
-    for first in range(0, size, step):
-        own = first // 8
-        at = first % 8
+    step = 8
+
+    def spread(x):
+        return jnp.broadcast_to(x, (8, width))
+
+    for own in range(size // 8):
+        first = size + own * step
         live = range(own, size // 8)
-        rows = [
-            jnp.broadcast_to(groups[own][at + k : at + k + 1], (8, width)) for k in range(step)
-        ]
+        rows = [spread(groups[own][k : k + 1]) for k in range(step)]
         cols = [
-            {
-                g: jnp.broadcast_to(
-                    groups[g][:, size + first + k : size + first + k + 1], (8, width)
-                )
-                for g in live
-            }
+            {g: spread(groups[g][:, first + k : first + k + 1]) for g in live}
             for k in range(step)
         ]
-        cross = [
-            [
-                jnp.broadcast_to(cols[m][own][at + k : at + k + 1], (8, width))
-                for m in range(step)
-            ]
-            for k in range(step)
-        ]
+        cross = {
+            (k, m): spread(cols[m][own][k : k + 1]) for k in range(step) for m in range(k + 1)
+        }
         for k in range(step):
-            inverse = 1.0 / cross[k][k]
-            pivots[own] = jnp.where(sub == at + k, cross[k][k], pivots[own])
+            inverse = 1.0 / cross[k, k]
+            pivots[own] = jnp.where(sub == k, cross[k, k], pivots[own])
+            factor = {later: cross[later, k] * inverse for later in range(k + 1, step)}
             for later in range(k + 1, step):
-                factor = cross[later][k] * inverse
-                rows[later] = rows[later] - factor * rows[k]
-                share = cross[k][later] * inverse
+                for m in range(k + 1, later + 1):
+                    cross[later, m] = cross[later, m] - factor[later] * cross[m, k]
+            for later in range(k + 1, step):
+                rows[later] = rows[later] - factor[later] * rows[k]
                 for g in live:
-                    cols[later][g] = cols[later][g] - share * cols[k][g]
-                for m in range(k + 1, step):
-                    cross[later][m] = cross[later][m] - factor * cross[k][m]
+                    cols[later][g] = cols[later][g] - factor[later] * cols[k][g]
             for g in live:
                 weight = cols[k][g] * inverse
                 if g == own:
-                    weight = jnp.where(sub > at + k, weight, 0.0)
+                    weight = jnp.where(sub > k, weight, 0.0)
                 groups[g] = groups[g] - weight * rows[k]
     scaled = [g / jnp.sqrt(p) for g, p in zip(groups, pivots)]
     return jnp.concatenate(scaled, axis=0)[:, :size]
 
 
 def kernel(
-    feats, samps, emb, bits, perm, gauss, scale, phase, basis, out, scores_out,
-    table, small, features, score_send, score_recv, proj, upd_send, upd_recv, grown,
-    gram_send, gram_recv,
-    s1, r1, s2, r2, s3, r3, s4, r4, s5, r5,
+    feats, samps, emb_in, bits_in, perm_in, gauss_in, scale_in, phase_in, basis_in,
+    proj_out, grown_out, gram_out,
+    emb, bits, perm, gauss, scale, phase, basis,
+    table, small, features, score_send, score_recv, proj, upd_send, upd_recv,
+    grown, quarters, grams,
+    s1, r1, s2, r2, s3, r3, s4, r4, s5, r5, s6, r6, loads, emb_loads, stores,
 ):
     me = lax.axis_index("feat")
     my = lax.axis_index("samp")
@@ -123,6 +117,26 @@
     order = basis.shape[0]
     chunk = rows // feats
     span = width // samps
+
+    def chunk_rows(slot):
+        return pl.ds(pl.multiple_of(slot * chunk, chunk), chunk)
+
+    def emb_load(slot):
+        where = chunk_rows(slot)
+        return pltpu.make_async_copy(emb_in.at[where, :], emb.at[where, :], emb_loads.at[slot])
+
+    pairs = (
+        (perm_in, perm), (bits_in, bits), (gauss_in, gauss), (scale_in, scale),
+        (phase_in, phase), (basis_in, basis),
+    )
+    parameters = [
+        pltpu.make_async_copy(source, place, loads.at[n])
+        for n, (source, place) in enumerate(pairs)
+    ]
+    for load in parameters:
+        load.start()
+    for d in range(1, feats + 1):
+        emb_load(lax.rem(me + d, feats)).start()
     barrier = pltpu.get_barrier_semaphore()
     for d in range(1, feats):
         pl.semaphore_signal(
@@ -133,6 +147,8 @@
             barrier, inc=1, device_id={"samp": lax.rem(my + d, samps)}, device_id_type=MESH
         )
 
+    for load in parameters:
+        load.wait()
     places = perm[...]
     base = parity_sign(lax.broadcasted_iota(jnp.int32, (128, width), 0) & places & 127).astype(
         jnp.bfloat16
@@ -150,8 +166,6 @@
     offset = phase[...] * (1.0 / (2.0 * math.pi))
     basis_low = basis[...].astype(jnp.bfloat16)
 
-    pl.semaphore_wait(barrier, feats + samps - 2)
-
     def copy(src, dst, send, recv, axis, to):
         return pltpu.make_async_remote_copy(
             src_ref=src, dst_ref=dst, send_sem=send, recv_sem=recv,
@@ -161,17 +175,19 @@
     def score_copy(to):
         return copy(score_send.at[to], score_recv.at[me], s1.at[to], r1.at[me], "feat", to)
 
-    def chunk_step(i, carry):
+    def chunk_scores(i):
         at = lax.rem(me + 1 + i, feats)
-        where = pl.ds(pl.multiple_of(at * chunk, chunk), chunk)
+        where = chunk_rows(at)
+        emb_load(at).wait()
         signed = emb[where, :] * signs
-        parts = []
-        for n in range(width // BLOCK):
-            cols = slice(n * BLOCK, (n + 1) * BLOCK)
-            first = jnp.dot(signed, table[:, cols], preferred_element_type=jnp.float32)
-            first = first.astype(jnp.bfloat16).astype(jnp.float32)
-            mixed = (first * gains[:, cols]).astype(jnp.bfloat16)
-            parts.append(jnp.dot(mixed, small[...], preferred_element_type=jnp.float32))
+        first = jnp.dot(signed, table[...], preferred_element_type=jnp.float32)
+        first = first.astype(jnp.bfloat16).astype(jnp.float32)
+        mixed = (first * gains).astype(jnp.bfloat16)
+        stacked = jnp.concatenate(
+            [mixed[:, n * BLOCK : (n + 1) * BLOCK] for n in range(width // BLOCK)], axis=0
+        )
+        stacked = jnp.dot(stacked, small[...], preferred_element_type=jnp.float32)
+        parts = [stacked[n * chunk : (n + 1) * chunk] for n in range(width // BLOCK)]
         for n, part in enumerate(transform(parts)):
             cols = slice(n * BLOCK, (n + 1) * BLOCK)
             turns = part * rate[:, cols] + offset[:, cols]
@@ -180,6 +196,10 @@
             basis_low, features[where, :], (((1,), (1,)), ((), ())),
             preferred_element_type=jnp.float32,
         )
+        return at
+
+    def chunk_step(i, carry):
+        at = chunk_scores(i)
 
         @pl.when(i < feats - 1)
         def _():
@@ -187,7 +207,10 @@
 
         return carry
 
-    lax.fori_loop(0, feats, chunk_step, 0)
+    to = chunk_scores(0)
+    pl.semaphore_wait(barrier, feats + samps - 2)
+    score_copy(to).start()
+    lax.fori_loop(1, feats, chunk_step, 0)
 
     total = score_send[me]
     for d in range(1, feats):
@@ -206,7 +229,7 @@
         proj_copy(me, lax.rem(me + d, feats)).start()
 
     def add_rows(slot, first):
-        where = pl.ds(pl.multiple_of(slot * chunk, chunk), chunk)
+        where = chunk_rows(slot)
         low = proj[slot].astype(jnp.bfloat16)
         for q in range(samps):
             term = jnp.dot(
@@ -226,8 +249,8 @@
 
     for d in range(1, samps):
         upd_copy(lax.rem(my + d, samps)).start()
-    for slot in range(feats):
-        scores_out[:, slot * chunk : (slot + 1) * chunk] = proj[slot]
+    proj_store = pltpu.make_async_copy(proj, proj_out, stores.at[0])
+    proj_store.start()
     total = upd_send[my]
     for d in range(1, samps):
         source = lax.rem(my + d, samps)
@@ -239,58 +262,97 @@
     own_cols = pl.ds(pl.multiple_of(my * span, span), span)
     grown[my] = basis[:, own_cols] + total * (1.0 / math.sqrt(rows * samps))
 
+    block = grown[my]
+    gram = lax.dot_general(
+        block, block, (((1,), (1,)), ((), ())), precision=HIGHEST,
+        preferred_element_type=jnp.float32,
+    )
+    half = order // 2
+    quarters[my] = jnp.concatenate([gram[:half], gram[half:]], axis=1)
+
+    def quarter_copy(slot, to):
+        return copy(quarters.at[slot], quarters.at[slot], s6.at[to], r6.at[slot], "samp", to)
+
     def grown_copy(slot, to):
         return copy(grown.at[slot], grown.at[slot], s4.at[to], r4.at[slot], "samp", to)
 
     for d in range(1, samps):
+        quarter_copy(my, lax.rem(my + d, samps)).start()
+    for d in range(1, samps):
         grown_copy(my, lax.rem(my + d, samps)).start()
-
-    def gram_of(slot):
-        block = grown[slot]
-        return lax.dot_general(
-            block, block, (((1,), (1,)), ((), ())), precision=HIGHEST,
-            preferred_element_type=jnp.float32,
-        )
-
-    gram = gram_of(my)
+    for d in range(1, samps):
+        source = lax.rem(my + d, samps)
+        quarter_copy(source, source).wait_recv()
+    packed = quarters[0]
+    for slot in range(1, samps):
+        packed = packed + quarters[slot]
+    grams[me] = packed
+
+    def gram_copy(slot, to):
+        return copy(grams.at[slot], grams.at[slot], s5.at[to], r5.at[slot], "feat", to)
+
+    for d in range(1, feats):
+        gram_copy(me, lax.rem(me + d, feats)).start()
     for d in range(1, samps):
         source = lax.rem(my + d, samps)
         grown_copy(source, source).wait_recv()
-        gram = gram + gram_of(source)
-
-    half = order // 2
-    packed = jnp.concatenate([gram[:half], gram[half:]], axis=1)
-    gram_send[...] = packed
-
-    def gram_copy(slot, to):
-        return copy(gram_send, gram_recv.at[slot], s5.at[to], r5.at[slot], "feat", to)
-
-    for d in range(1, feats):
-        gram_copy(me, lax.rem(me + d, feats)).start()
-    gram_recv[me] = packed
+    grown_store = pltpu.make_async_copy(grown, grown_out, stores.at[1])
+    grown_store.start()
     for d in range(1, feats):
         source = lax.rem(me + d, feats)
         gram_copy(source, source).wait_recv()
-    packed = gram_recv[0]
+    packed = grams[0]
     for slot in range(1, feats):
-        packed = packed + gram_recv[slot]
-    packed = packed * (1.0 / (width * feats))
-    gram = jnp.concatenate([packed[:, :order], packed[:, order:]], axis=0)
-    inverse = inverse_factor(gram)
-    for q in range(samps):
-        out[:, q * span : (q + 1) * span] = jnp.dot(
-            inverse, grown[q], precision=HIGHEST, preferred_element_type=jnp.float32
-        )
-
+        packed = packed + grams[slot]
+    gram_out[...] = packed * (1.0 / (width * feats))
     for d in range(1, feats):
         to = lax.rem(me + d, feats)
         score_copy(to).wait_send()
         proj_copy(me, to).wait_send()
         gram_copy(me, to).wait_send()
+    proj_store.wait()
+    grown_store.wait()
     for d in range(1, samps):
         to = lax.rem(my + d, samps)
         upd_copy(to).wait_send()
+        quarter_copy(my, to).wait_send()
         grown_copy(my, to).wait_send()
+
+
+def finish(
+    proj_in, grown_in, packed, out, scores_out, proj, grown, result, loads, out_sems, score_sems
+):
+    feats, order, chunk = proj.shape
+    samps, _, span = grown.shape
+    proj_load = pltpu.make_async_copy(proj_in, proj, loads.at[0])
+    grown_load = pltpu.make_async_copy(grown_in, grown, loads.at[1])
+    proj_load.start()
+    grown_load.start()
+    proj_load.wait()
+    stores = [
+        pltpu.make_async_copy(
+            proj.at[slot], scores_out.at[:, slot * chunk : (slot + 1) * chunk],
+            score_sems.at[slot],
+        )
+        for slot in range(feats)
+    ]
+    for store in stores:
+        store.start()
+    halves = packed[...]
+    gram = jnp.concatenate([halves[:, :order], halves[:, order:]], axis=0)
+    inverse = inverse_factor(gram)
+    grown_load.wait()
+    for q in range(samps):
+        result[q] = jnp.dot(
+            inverse, grown[q], precision=HIGHEST, preferred_element_type=jnp.float32
+        )
+        store = pltpu.make_async_copy(
+            result.at[q], out.at[:, q * span : (q + 1) * span], out_sems.at[q]
+        )
+        store.start()
+        stores.append(store)
+    for store in stores:
+        store.wait()
 
 
 def fused(feats, samps, embeddings, sign_bits, perms, gauss, scale, phase, basis):
@@ -299,16 +361,25 @@
     chunk, span = rows // feats, width // samps
     line = (1, width)
     whole = pl.BlockSpec(memory_space=pltpu.VMEM)
+    far = pl.BlockSpec(memory_space=pltpu.HBM)
     f32, bf16, dma = jnp.float32, jnp.bfloat16, pltpu.SemaphoreType.DMA
-    return pl.pallas_call(
+    proj, grown, packed = pl.pallas_call(
         functools.partial(kernel, feats, samps),
         out_shape=(
-            jax.ShapeDtypeStruct((order, width), f32),
-            jax.ShapeDtypeStruct((order, rows), f32),
+            jax.ShapeDtypeStruct((feats, order, chunk), f32),
+            jax.ShapeDtypeStruct((samps, order, span), f32),
+            jax.ShapeDtypeStruct((order // 2, 2 * order), f32),
         ),
-        in_specs=[whole] * 7,
-        out_specs=(whole, whole),
+        in_specs=[far] * 7,
+        out_specs=(far, far, whole),
         scratch_shapes=[
+            pltpu.VMEM((rows, width), bf16),
+            pltpu.VMEM(line, jnp.int32),
+            pltpu.VMEM(line, jnp.int32),
+            pltpu.VMEM(line, f32),
+            pltpu.VMEM(line, f32),
+            pltpu.VMEM(line, f32),
+            pltpu.VMEM((order, width), f32),
             pltpu.VMEM((width, width), bf16),
             pltpu.VMEM((BLOCK, BLOCK), bf16),
             pltpu.VMEM((rows, width), bf16),
@@ -318,20 +389,38 @@
             pltpu.VMEM((samps, order, span), f32),
             pltpu.VMEM((samps, order, span), f32),
             pltpu.VMEM((samps, order, span), f32),
-            pltpu.VMEM((order // 2, 2 * order), f32),
+            pltpu.VMEM((samps, order // 2, 2 * order), f32),
             pltpu.VMEM((feats, order // 2, 2 * order), f32),
         ]
         + [dma((feats,))] * 4
         + [dma((samps,))] * 4
-        + [dma((feats,))] * 2,
+        + [dma((feats,))] * 2
+        + [dma((samps,))] * 2
+        + [dma((6,)), dma((feats,)), dma((2,))],
         compiler_params=pltpu.CompilerParams(
-            collective_id=0, has_side_effects=True, vmem_limit_bytes=40 << 20
+            collective_id=0, has_side_effects=True, vmem_limit_bytes=64 << 20
         ),
         name="oja",
     )(
         embeddings, sign_bits.reshape(line), perms.reshape(line), gauss.reshape(line),
         scale.reshape(line), phase.reshape(line), basis,
     )
+    return pl.pallas_call(
+        finish,
+        out_shape=(
+            jax.ShapeDtypeStruct((order, width), f32),
+            jax.ShapeDtypeStruct((order, rows), f32),
+        ),
+        in_specs=[far, far, whole],
+        out_specs=(far, far),
+        scratch_shapes=[
+            pltpu.VMEM((feats, order, chunk), f32),
+            pltpu.VMEM((samps, order, span), f32),
+            pltpu.VMEM((samps, order, span), f32),
+            dma((2,)), dma((samps,)), dma((feats,)),
+        ],
+        name="finish",
+    )(proj, grown, packed)
 
 
 def sylvester(width):

time: 46.8 us -> 40.7 us (0.87)
  local copies, waits for them, and re-layouts: 7.37 us -> 0 us
  Pallas kernels: 38.4 us -> 39.8 us
    unnamed x16 -> x0, local copies, waits for them, and re-layouts: 7.37 us -> none
    pallas_call x0 -> x1, Pallas kernels: none -> 4.74 us  [fused(): pl.pallas_call(finish, out_shape=(jax.ShapeDtypeStruct((order, width), f3...]
    pallas_call x1, Pallas kernels: 38.4 us -> 35.1 us  [fused(): pl.pallas_call(functools.partial(kernel, feats, samps), out_shape=(jax.Sh...]
where the time goes in v2:
time: 40.7 us; the launch traced here: 40.4 us
  Pallas kernels  39.8 us (98%)
  between operations  0.64 us (2%)
    pallas_call x1, Pallas kernels, fused(): pl.pallas_call(functools.partial(kernel, feats, samps), out_shape=(jax.Sh...  35.1 us
    pallas_call x1, Pallas kernels, fused(): pl.pallas_call(finish, out_shape=(jax.ShapeDtypeStruct((order, width), f3...  4.74 us

profile of v2, /device:TPU:0, one launch (start us, length us, event | category | flops | bytes accessed | tf_op | source)
XLA Modules:
  0.0 40.4 jit_solution(1811164545378055774)
XLA Ops:
  0.6 35.1 %oja.1 = (f32[4,64,256]{2,1,0:T(8,128)}, f32[4,64,256]{2,1,0:T(8,128)}, f32[32,128]{1,0:T(8,128)}) custom-call(bf16[1024,1024]{1,0:T(8,128)(2,1)} %emb_in.1, s32[1,1024]{1,0:T(1,128)} %bitcast.4, s32[1,1024]{1,0:T(1,128)} %perm_in.1, f32[1,1024]{1,0:T(1,128)} %bitcast.5, f32[1,1024]{1,0:T(1,128)} %bitcast.6, f32[1,1024]{1,0:T(1,128)} %bitcast.7, ...), custom_call_target="tpu_custom_call" | custom-call | tf_op jit(solution)/shard_map/oja/pallas_call | solution.py:366
  35.7 4.7 %finish.1 = (f32[64,1024]{1,0:T(8,128)}, f32[64,1024]{1,0:T(8,128)}) custom-call(f32[4,64,256]{2,1,0:T(8,128)} %get-tuple-element.5.proj_in, f32[4,64,256]{2,1,0:T(8,128)} %get-tuple-element.6.grown_in, f32[32,128]{1,0:T(8,128)} %get-tuple-element.7.packed), custom_call_target="tpu_custom_call" | custom-call | tf_op jit(solution)/shard_map/finish/pallas_call | solution.py:408

commit v3 on v2

--- a/solution.py
+++ b/solution.py
@@ -52,6 +52,14 @@
         blocks = result
         stride *= 2
     return blocks
+
+
+def split(x):
+    high = x.astype(jnp.bfloat16)
+    rest = x - high.astype(jnp.float32)
+    middle = rest.astype(jnp.bfloat16)
+    low = (rest - middle.astype(jnp.float32)).astype(jnp.bfloat16)
+    return high, middle, low
 
 
 def inverse_factor(gram):
@@ -226,9 +234,12 @@
         return copy(proj.at[slot], proj.at[slot], s2.at[to], r2.at[slot], "feat", to)
 
     for d in range(1, feats):
-        proj_copy(me, lax.rem(me + d, feats)).start()
-
-    def add_rows(slot, first):
+        proj_copy(me, lax.rem(me + feats - d, feats)).start()
+
+    def upd_copy(to):
+        return copy(upd_send.at[to], upd_recv.at[my], s3.at[to], r3.at[my], "samp", to)
+
+    def add_rows(slot, first, last):
         where = chunk_rows(slot)
         low = proj[slot].astype(jnp.bfloat16)
         for q in range(samps):
@@ -237,18 +248,18 @@
                 preferred_element_type=jnp.float32,
             )
             upd_send[q] = term if first else upd_send[q] + term
-
-    add_rows(me, True)
+            if last:
+
+                @pl.when(my != q)
+                def _():
+                    upd_copy(q).start()
+
+    add_rows(me, True, False)
     for d in range(1, feats):
         source = lax.rem(me + d, feats)
         proj_copy(source, source).wait_recv()
-        add_rows(source, False)
-
-    def upd_copy(to):
-        return copy(upd_send.at[to], upd_recv.at[my], s3.at[to], r3.at[my], "samp", to)
-
-    for d in range(1, samps):
-        upd_copy(lax.rem(my + d, samps)).start()
+        add_rows(source, False, d == feats - 1)
+
     proj_store = pltpu.make_async_copy(proj, proj_out, stores.at[0])
     proj_store.start()
     total = upd_send[my]
@@ -279,8 +290,6 @@
     for d in range(1, samps):
         quarter_copy(my, lax.rem(my + d, samps)).start()
     for d in range(1, samps):
-        grown_copy(my, lax.rem(my + d, samps)).start()
-    for d in range(1, samps):
         source = lax.rem(my + d, samps)
         quarter_copy(source, source).wait_recv()
     packed = quarters[0]
@@ -293,6 +302,8 @@
 
     for d in range(1, feats):
         gram_copy(me, lax.rem(me + d, feats)).start()
+    for d in range(1, samps):
+        grown_copy(my, lax.rem(my + d, samps)).start()
     for d in range(1, samps):
         source = lax.rem(my + d, samps)
         grown_copy(source, source).wait_recv()
@@ -341,11 +352,13 @@
     halves = packed[...]
     gram = jnp.concatenate([halves[:, :order], halves[:, order:]], axis=0)
     inverse = inverse_factor(gram)
+    high, middle, low = split(inverse)
+    left = jnp.concatenate([high, high, middle, high, middle, low], axis=1)
     grown_load.wait()
     for q in range(samps):
-        result[q] = jnp.dot(
-            inverse, grown[q], precision=HIGHEST, preferred_element_type=jnp.float32
-        )
+        high, middle, low = split(grown[q])
+        right = jnp.concatenate([high, middle, high, low, middle, high], axis=0)
+        result[q] = jnp.dot(left, right, preferred_element_type=jnp.float32)
         store = pltpu.make_async_copy(
             result.at[q], out.at[:, q * span : (q + 1) * span], out_sems.at[q]
         )

time: 40.7 us -> 40.3 us (level)
  Pallas kernels: 39.8 us -> 39.1 us
    pallas_call x1, Pallas kernels: 35.1 us -> 34.3 us  [fused(): pl.pallas_call(functools.partial(kernel, feats, samps), out_shape=(jax.Sh...]
where the time goes in v3:
time: 40.3 us; the launch traced here: 39.7 us
  Pallas kernels  39.1 us (97%)
  between operations  0.64 us (2%)
    pallas_call x1, Pallas kernels, fused(): pl.pallas_call(functools.partial(kernel, feats, samps), out_shape=(jax.Sh...  34.3 us
    pallas_call x1, Pallas kernels, fused(): pl.pallas_call(finish, out_shape=(jax.ShapeDtypeStruct((order, width), f3...  4.73 us

profile of v3, /device:TPU:0, one launch (start us, length us, event | category | flops | bytes accessed | tf_op | source)
XLA Modules:
  0.0 39.7 jit_solution(15584896462316215026)
XLA Ops:
  0.6 34.3 %oja.1 = (f32[4,64,256]{2,1,0:T(8,128)}, f32[4,64,256]{2,1,0:T(8,128)}, f32[32,128]{1,0:T(8,128)}) custom-call(bf16[1024,1024]{1,0:T(8,128)(2,1)} %emb_in.1, s32[1,1024]{1,0:T(1,128)} %bitcast.4, s32[1,1024]{1,0:T(1,128)} %perm_in.1, f32[1,1024]{1,0:T(1,128)} %bitcast.5, f32[1,1024]{1,0:T(1,128)} %bitcast.6, f32[1,1024]{1,0:T(1,128)} %bitcast.7, ...), custom_call_target="tpu_custom_call" | custom-call | tf_op jit(solution)/shard_map/oja/pallas_call | solution.py:379
  35.0 4.7 %finish.1 = (f32[64,1024]{1,0:T(8,128)}, f32[64,1024]{1,0:T(8,128)}) custom-call(f32[4,64,256]{2,1,0:T(8,128)} %get-tuple-element.5.proj_in, f32[4,64,256]{2,1,0:T(8,128)} %get-tuple-element.6.grown_in, f32[32,128]{1,0:T(8,128)} %get-tuple-element.7.packed), custom_call_target="tpu_custom_call" | custom-call | tf_op jit(solution)/shard_map/finish/pallas_call | solution.py:421
